TPU v7x, 32 devices: a whole 2x2x4 slice. The times are simulated.
32 devices in a mesh: tm: 2 (over x), diamond: 2 (over y), tile: 8 (over z, core).
Axes of the slice: x: 2, y: 2, z: 4, core: 2. Of those that a mesh axis runs over, the one named last changes fastest.
Arguments:
- activations: bfloat16 [8, 2, 32, 64, 256], P('tm', 'diamond', 'tile'), may hold values from -6 to 6
- upstream: bfloat16 [8, 2, 32, 64, 256], P('tm', 'diamond', 'tile'), may hold values from -16 to 16
- hex_weight: bfloat16 [7, 64, 64], replicated, may hold values from -0.25 to 0.25
- time_weight: bfloat16 [3, 64, 64], replicated, may hold values from -0.4375 to 0.4375
- left_map: int32 [2, 32], replicated, may hold values from 0 to 31, each once within a row
- right_map: int32 [2, 32], replicated, may hold values from 0 to 31, each once within a row
Outputs:
- grad_input: bfloat16 [8, 2, 32, 64, 256], P('tm', 'diamond', 'tile')
- grad_hex: float32 [7, 64, 64], replicated
- grad_time: float32 [3, 64, 64], replicated
Inputs may be any that keep to these rules, and one draw needn't show every extreme that they name: Each row of left_map holds every number of 0 to 31 once. Each row of right_map holds every number of 0 to 31 once.
All inputs are finite; a program needn't handle non-finite values.
Results may differ from a plain program's by a relative error of at most 0.0035.
Values may be sent and summed in bfloat16 or wider, within the bound.
A program may use at most 64 MiB of HBM per device.

v0:
```python
import jax
import jax.numpy as jnp
from jax import lax
from jax.sharding import PartitionSpec as P

OFFSETS = ((0, 0), (0, 1), (0, -1), (1, 0), (-1, 0), (1, -1), (-1, 1))


def from_behind(block, axis, distance):
    devices = range(lax.axis_size(axis))
    route = [((i - distance) % len(devices), i) for i in devices]
    return lax.ppermute(block, axis, route)


def with_halo(x, sides, width):
    for axis, dim in sides:
        size, length = (lax.axis_size(axis), x.shape[dim])
        up = [(i, (i + 1) % size) for i in range(size - 1)]
        down = [(j, i) for i, j in up]
        last = lax.slice_in_dim(x, length - width, length, axis=dim)
        initial = lax.slice_in_dim(x, 0, width, axis=dim)
        before = lax.ppermute(last, axis, up)
        after = lax.ppermute(initial, axis, down)
        x = jnp.concatenate([before, x, after], axis=dim)
    return x


def passed_along(block, axis, distance):
    devices = range(lax.axis_size(axis))
    route = [(i - distance, i) for i in devices if i - distance in devices]
    return lax.ppermute(block, axis, route)


def silu_slope(hidden):
    sigmoid = jax.nn.sigmoid(hidden)
    return sigmoid * (1.0 + hidden * (1.0 - sigmoid))


def shards(activations, upstream, hex_weight, time_weight, left_map, right_map):
    field = activations[:, 0]
    cotangent = upstream[:, 0]
    frames, tile_rows, channels, columns = field.shape
    chart = lax.axis_index("diamond")
    first_row = lax.axis_index("tile") * tile_rows
    chart_rows = tile_rows * lax.axis_size("tile")
    own_left = lax.dynamic_slice(left_map, (chart, first_row), (1, tile_rows))[0]
    own_right = lax.dynamic_slice(right_map, (chart, first_row), (1, tile_rows))[0]
    strips = (
        lax.all_gather(field[..., 0], "tile", axis=1, tiled=True),
        lax.all_gather(field[..., columns - 1], "tile", axis=1, tiled=True),
    )
    prev_right = from_behind(strips[1], "diamond", 1)
    next_left = from_behind(strips[0], "diamond", -1)
    ghost_left = jnp.take(prev_right, own_left, axis=1)
    ghost_right = jnp.take(next_left, own_right, axis=1)
    widened = jnp.concatenate([ghost_left[..., None], field, ghost_right[..., None]], axis=-1)
    depth = 1
    margin = depth - 1
    span_rows = tile_rows + 2 * margin
    padded = with_halo(widened, (("tile", 1),), depth)
    hidden = jnp.zeros((frames, span_rows, channels, columns), jnp.float32)
    for number, (step_row, step_col) in enumerate(OFFSETS):
        window = padded[
            :, 1 + step_row : 1 + step_row + span_rows, :, 1 + step_col : 1 + step_col + columns
        ]
        hidden = hidden + jnp.einsum(
            "frcx,cd->frdx", window, hex_weight[number], preferred_element_type=jnp.float32
        )
    active = jax.nn.silu(hidden).astype(jnp.bfloat16)
    framed = with_halo(cotangent, (("tm", 0),), 1)
    grad_act = jnp.zeros((frames, span_rows, channels, columns), jnp.float32)
    time_terms = []
    for number in range(3):
        shifted = framed[2 - number : 2 - number + frames]
        grad_act = grad_act + jnp.einsum(
            "frdx,cd->frcx", shifted, time_weight[number], preferred_element_type=jnp.float32
        )
        time_terms.append(
            jnp.einsum("frcx,frdx->cd", active, shifted, preferred_element_type=jnp.float32)
        )
    grad_wide = (grad_act * silu_slope(hidden)).astype(jnp.bfloat16)
    hex_terms = []
    for number, (step_row, step_col) in enumerate(OFFSETS):
        begin = 1 + margin + step_row
        window = padded[:, begin : begin + tile_rows, :, 1 + step_col : 1 + step_col + columns]
        hex_terms.append(
            jnp.einsum("frcx,frdx->cd", window, grad_wide, preferred_element_type=jnp.float32)
        )
    spread = jnp.zeros((frames, tile_rows + 2, channels, columns + 2), jnp.float32)
    for number, (step_row, step_col) in enumerate(OFFSETS):
        spread = spread.at[
            :, 1 + step_row : 1 + step_row + tile_rows, :, 1 + step_col : 1 + step_col + columns
        ].add(
            jnp.einsum(
                "frdx,cd->frcx", grad_wide, hex_weight[number], preferred_element_type=jnp.float32
            )
        )
    from_below = passed_along(spread[:, 0].astype(jnp.bfloat16), "tile", -1).astype(jnp.float32)
    from_above = passed_along(spread[:, tile_rows + 1].astype(jnp.bfloat16), "tile", 1).astype(
        jnp.float32
    )
    owned = spread[:, 1 : tile_rows + 1]
    owned = owned.at[:, 0].add(from_above)
    owned = owned.at[:, tile_rows - 1].add(from_below)
    total = cotangent.astype(jnp.float32) + owned[..., 1 : columns + 1]
    left_grad = owned[..., 0]
    right_grad = owned[..., columns + 1]
    strip_left = (
        jnp.zeros((frames, chart_rows, channels), jnp.float32).at[:, own_left].set(left_grad)
    )
    strip_right = (
        jnp.zeros((frames, chart_rows, channels), jnp.float32).at[:, own_right].set(right_grad)
    )
    moved_left = from_behind(strip_left.astype(jnp.bfloat16), "diamond", -1).astype(
        strip_left.dtype
    )
    moved_right = from_behind(strip_right.astype(jnp.bfloat16), "diamond", 1).astype(
        strip_right.dtype
    )
    into_last, into_first = (
        lax.psum_scatter(
            moved_left.astype(jnp.bfloat16), "tile", scatter_dimension=1, tiled=True
        ).astype(jnp.float32),
        lax.psum_scatter(
            moved_right.astype(jnp.bfloat16), "tile", scatter_dimension=1, tiled=True
        ).astype(jnp.float32),
    )
    total = total.at[..., columns - 1].add(into_last)
    total = total.at[..., 0].add(into_first)
    hex_local = jnp.stack(hex_terms)
    time_local = jnp.stack(time_terms)
    grad_hex, grad_time = lax.psum((hex_local, time_local), ("tm", "diamond", "tile"))
    return (total.astype(jnp.bfloat16)[:, None], grad_hex, grad_time)


def solution(mesh):
    in_specs = (
        P("tm", "diamond", "tile", None, None),
        P("tm", "diamond", "tile", None, None),
        P(),
        P(),
        P(),
        P(),
    )
    out_specs = (P("tm", "diamond", "tile", None, None), P(), P())
    return jax.shard_map(shards, mesh=mesh, in_specs=in_specs, out_specs=out_specs, check_vma=False)
```

profile of v0, /device:TPU:0, one launch (start us, length us, event | category | flops | bytes accessed | tf_op | source)
XLA Modules:
  0.0 317.2 jit_solution(10565177064639616680)
XLA Ops:
  8.4 25.1 %all-gather = bf16[4,32,64,1]{3,2,1,0:T(8,128)(2,1)S(1)} all-gather(bf16[4,4,64,1]{3,2,1,0:T(8,128)(2,1)S(1)} %get-tuple-element.164), channel_id=2, replica_groups=mesh['tm'=2,'diamond'=2,'tile'=8] {'tile'}, dimensions={1}, use_global_device_ids=true | all-gather | bytes 18432 | tf_op jit(solution)/shard_map/all_gather | solution.py:49
  34.6 1.6 collective-permute-start.2
  36.2 22.7 %all-gather.1 = bf16[4,32,64,1]{3,2,1,0:T(8,128)(2,1)S(1)} all-gather(bf16[4,4,64,1]{3,2,1,0:T(8,128)(2,1)S(1)} %get-tuple-element.163), channel_id=3, replica_groups=mesh['tm'=2,'diamond'=2,'tile'=8] {'tile'}, dimensions={1}, use_global_device_ids=true | all-gather | bytes 18432 | tf_op jit(solution)/shard_map/all_gather | solution.py:50
  61.2 4.2 %collective-permute-start.1 = (bf16[1,4,64,256]{3,2,1,0:T(8,128)(2,1)}, bf16[1,4,64,256]{3,2,1,0:T(8,128)(2,1)}, u32[]{:S(2)}, u32[]{:S(2)}) collective-permute-start(bf16[1,4,64,256]{3,2,1,0:T(8,128)(2,1)} %get-tuple-element.162), channel_id=1, source_target_pairs={{0,16},{1,17},{2,18},{3,19},{4,20},{5,21},{6,22},{7,23},{8,24},{9,... | collective-permute-start | bytes 393224 | tf_op jit(solution)/shard_map/ppermute | solution.py:22
  69.1 2.7 and_reduce_fusion
  77.7 3.2 %collective-permute-start.5 = (bf16[4,1,64,258]{3,2,1,0:T(8,128)(2,1)S(1)}, bf16[4,1,64,258]{3,2,1,0:T(8,128)(2,1)S(1)}, u32[]{:S(2)}, u32[]{:S(2)}) collective-permute-start(bf16[4,1,64,258]{3,2,1,0:T(8,128)(2,1)S(1)} %get-tuple-element.160), channel_id=1, source_target_pairs={{0,1},{1,2},{2,3},{3,4},{4,5},{5,6},{6,7},{8,9},{9,10},{10,11},{11... | collective-permute-start | bytes 396296 | tf_op jit(solution)/shard_map/ppermute | solution.py:22
  86.0 1.5 fusion.15
  90.5 7.1 %scatter-add.39 = f32[4,6,64,258]{3,2,0,1:T(8,128)S(1)} dynamic-update-slice(f32[4,6,64,258]{3,2,0,1:T(8,128)S(1)} %scatter-add.36, f32[4,4,64,256]{3,2,0,1:T(8,128)} %fusion.9, s32[]{:T(128)} %constant.332.clone.1, s32[]{:T(128)} %constant.338.clone.1, s32[]{:T(128)} %constant.332.clone.1, s32[]{:T(128)} %constant.333.clone.1) | dynamic-update-slice | bytes 2097156 | tf_op jit(solution)/shard_map/scatter-add | solution.py:93
  99.3 7.1 %scatter-add.41 = f32[4,6,64,258]{3,2,0,1:T(8,128)S(1)} dynamic-update-slice(f32[4,6,64,258]{3,2,0,1:T(8,128)S(1)} %fusion.11, f32[4,4,64,256]{3,2,0,1:T(8,128)} %fusion.12, s32[]{:T(128)} %constant.332.clone.1, s32[]{:T(128)} %constant.333.clone.1, s32[]{:T(128)} %constant.332.clone.1, s32[]{:T(128)} %constant.338.clone.1) | dynamic-update-slice | bytes 2097156 | tf_op jit(solution)/shard_map/scatter-add | solution.py:93
  106.3 2.7 add_select_fusion.1
  109.0 7.8 %scatter-add.44 = f32[4,6,64,258]{3,2,0,1:T(8,128)S(1)} dynamic-update-slice(f32[4,6,64,258]{3,2,0,1:T(8,128)S(1)} %scatter-add.41, f32[4,4,64,256]{3,2,0,1:T(8,128)} %add_select_fusion.1, s32[]{:T(128)} %constant.332.clone.1, s32[]{:T(128)S(1)} %bitcast.366, s32[]{:T(128)} %constant.332.clone.1, s32[]{:T(128)} %bitcast.61) | dynamic-update-slice | bytes 2097156 | tf_op jit(solution)/shard_map/scatter-add | solution.py:93
  117.1 3.2 add_select_fusion
  120.3 8.4 %scatter-add.46 = f32[4,6,64,258]{3,2,0,1:T(8,128)S(1)} dynamic-update-slice(f32[4,6,64,258]{3,2,0,1:T(8,128)S(1)} %fusion.14, f32[4,4,64,256]{3,2,0,1:T(8,128)} %add_select_fusion, s32[]{:T(128)} %constant.332.clone.1, s32[]{:T(128)} %bitcast.66, s32[]{:T(128)} %constant.332.clone.1, s32[]{:T(128)} %bitcast.67) | dynamic-update-slice | bytes 2097156 | tf_op jit(solution)/shard_map/scatter-add | solution.py:93
  138.6 1.8 slice_bitcast_fusion.1
  140.4 4.4 %collective-permute-start.6 = (bf16[4,64,258]{2,1,0:T(8,128)(2,1)}, bf16[4,64,258]{2,1,0:T(8,128)(2,1)}, u32[]{:S(2)}, u32[]{:S(2)}) collective-permute-start(bf16[4,64,258]{2,1,0:T(8,128)(2,1)} %get-tuple-element.156), channel_id=1, source_target_pairs={{0,1},{1,2},{2,3},{3,4},{4,5},{5,6},{6,7},{8,9},{9,10},{10,11},{11... | collective-permute-start | bytes 396296 | tf_op jit(solution)/shard_map/ppermute | solution.py:31
  148.7 45.7 %psum.15 = f32[3,64,64]{2,1,0:T(8,128)} all-reduce(f32[3,64,64]{2,1,0:T(8,128)S(1)} %pad_maximum_fusion.16), channel_id=1, replica_groups=mesh['tm'=2,'diamond'=2,'tile'=8] {'tm','diamond','tile'}, use_global_device_ids=true, to_apply=%region_7.9 | all-reduce | flops 12288 | bytes 98304 | tf_op jit(solution)/shard_map/psum | solution.py:132
  194.3 71.3 %all-reduce.6.cloned.1.call-done = f32[7,64,64]{1,2,0:T(8,128)} async-done(((f32[7,64,64]{1,2,0:T(8,128)}), f32[7,64,64]{1,2,0:T(8,128)}) %all-reduce.6.cloned.1.call-update) | async-done | bytes 114704 | tf_op jit(solution)/shard_map/psum | solution.py:132
  265.6 1.8 copy.133
  267.4 1.7 fusion.33
  269.1 1.5 copy.119
  273.0 1.5 collective-permute-start.8
  277.2 1.9 collective-permute-done.9
  279.1 26.9 %all-reduce.3 = (bf16[4,32,64]{2,0,1:T(4,128)(2,1)S(1)}, bf16[4,32,64]{2,0,1:T(4,128)(2,1)S(1)}) all-reduce(bf16[4,32,64]{2,0,1:T(4,128)(2,1)S(1)} %collective-permute-done.8, bf16[4,32,64]{2,0,1:T(4,128)(2,1)S(1)} %collective-permute-done.9), channel_id=4, replica_groups=mesh['tm'=2,'diamond'=2,'tile'=8] {'tile'}, use_global_device_ids=true, to_apply=%region_3.5.clone | all-reduce | flops 16384 | bytes 65536
  306.8 1.9 scatter-add.51
  (124 shorter events, 44.2 us)
Async XLA Ops:
  7.2 258.5 %all-reduce.6.cloned.1.call-start = ((), (), s32[]{:S(2)}) async-start(), calls=%async_computation | async-start | bytes 458752 | tf_op jit(solution)/shard_map/psum | solution.py:132
  34.6 38.7 %collective-permute-start.2 = (bf16[4,32,64]{2,0,1:T(4,128)(2,1)S(1)}, bf16[4,32,64]{2,0,1:T(4,128)(2,1)S(1)}, u32[]{:S(2)}, u32[]{:S(2)}) collective-permute-start(bf16[4,32,64]{2,0,1:T(4,128)(2,1)S(1)} %bitcast.359), channel_id=1, source_target_pairs={{8,0},{0,8},{9,1},{1,9},{10,2},{2,10},{11,3},{3,11},{12,4},{4,12},... | collective-permute-start | bytes 49160 | tf_op jit(solution)/shard_map/ppermute | solution.py:12
  36.1 24.3 %copy-start.1 = (bf16[4,1,4,64,256]{4,3,2,1,0:T(8,128)(2,1)S(1)}, bf16[4,1,4,64,256]{4,3,2,1,0:T(8,128)(2,1)}, u32[]{:S(2)}) copy-start(bf16[4,1,4,64,256]{4,3,2,1,0:T(8,128)(2,1)} %param.31) | copy-start | bytes 1572868
  36.1 30.6 %copy-start.14 = (s32[2,32]{1,0:T(2,128)S(1)}, s32[2,32]{1,0:T(2,128)}, u32[]{:S(2)}) copy-start(s32[2,32]{1,0:T(2,128)} %param.35) | copy-start | bytes 772
  36.2 30.6 %copy-start.15 = (s32[2,32]{1,0:T(2,128)S(1)}, s32[2,32]{1,0:T(2,128)}, u32[]{:S(2)}) copy-start(s32[2,32]{1,0:T(2,128)} %param.34) | copy-start | bytes 772
  58.9 10.3 %copy-start.16 = (s32[4]{0:T(128)S(1)}, s32[4]{0:T(128)}, u32[]{:S(2)}) copy-start(s32[4]{0:T(128)} %constant.340.clone.1) | copy-start | bytes 52
  58.9 13.0 %copy-start.17 = (u32[32]{0:T(128)S(1)}, u32[32]{0:T(128)}, u32[]{:S(2)}) copy-start(u32[32]{0:T(128)} %constant.350) | copy-start | bytes 388
  58.9 16.2 %copy-start = (bf16[4,1,4,64,256]{4,3,2,1,0:T(8,128)(2,1)S(1)}, bf16[4,1,4,64,256]{4,3,2,1,0:T(8,128)(2,1)}, u32[]{:S(2)}) copy-start(bf16[4,1,4,64,256]{4,3,2,1,0:T(8,128)(2,1)} %param.30) | copy-start | bytes 1572868
  59.9 14.3 %collective-permute-start.3 = (bf16[4,32,64]{2,0,1:T(4,128)(2,1)S(1)}, bf16[4,32,64]{2,0,1:T(4,128)(2,1)S(1)}, u32[]{:S(2)}, u32[]{:S(2)}) collective-permute-start(bf16[4,32,64]{2,0,1:T(4,128)(2,1)S(1)} %bitcast.358), channel_id=1, source_target_pairs={{8,0},{0,8},{9,1},{1,9},{10,2},{2,10},{11,3},{3,11},{12,4},{4,12},... | collective-permute-start | bytes 49160 | tf_op jit(solution)/shard_map/ppermute | solution.py:12
  61.2 14.2 %copy-start.12 = (bf16[7,64,64]{2,1,0:T(8,128)(2,1)S(1)}, bf16[7,64,64]{2,1,0:T(8,128)(2,1)}, u32[]{:S(2)}) copy-start(bf16[7,64,64]{2,1,0:T(8,128)(2,1)} %param.32) | copy-start | bytes 172036
  61.2 20.0 %collective-permute-start.1 = (bf16[1,4,64,256]{3,2,1,0:T(8,128)(2,1)}, bf16[1,4,64,256]{3,2,1,0:T(8,128)(2,1)}, u32[]{:S(2)}, u32[]{:S(2)}) collective-permute-start(bf16[1,4,64,256]{3,2,1,0:T(8,128)(2,1)} %get-tuple-element.162), channel_id=1, source_target_pairs={{0,16},{1,17},{2,18},{3,19},{4,20},{5,21},{6,22},{7,23},{8,24},{9,... | collective-permute-start | bytes 393224 | tf_op jit(solution)/shard_map/ppermute | solution.py:22
  65.4 20.6 %collective-permute-start = (bf16[1,4,64,256]{3,2,1,0:T(8,128)(2,1)}, bf16[1,4,64,256]{3,2,1,0:T(8,128)(2,1)}, u32[]{:S(2)}, u32[]{:S(2)}) collective-permute-start(bf16[1,4,64,256]{3,2,1,0:T(8,128)(2,1)} %get-tuple-element.161), channel_id=1, source_target_pairs={{16,0},{17,1},{18,2},{19,3},{20,4},{21,5},{22,6},{23,7},{24,8},{25... | collective-permute-start | bytes 393224 | tf_op jit(solution)/shard_map/ppermute | solution.py:23
  74.2 8.3 %copy-start.7 = (bf16[4,4,64,1]{3,2,1,0:T(8,128)(2,1)}, bf16[4,4,64,1]{3,2,1,0:T(8,128)(2,1)S(1)}, u32[]{:S(2)}) copy-start(bf16[4,4,64,1]{3,2,1,0:T(8,128)(2,1)S(1)} %copy.92) | copy-start | bytes 6148
  75.1 7.4 %copy-start.9 = (bf16[4,4,64,1]{3,2,1,0:T(8,128)(2,1)}, bf16[4,4,64,1]{3,2,1,0:T(8,128)(2,1)S(1)}, u32[]{:S(2)}) copy-start(bf16[4,4,64,1]{3,2,1,0:T(8,128)(2,1)S(1)} %copy.96) | copy-start | bytes 6148
  76.2 5.0 %copy-start.13 = (bf16[3,64,64]{2,1,0:T(8,128)(2,1)S(1)}, bf16[3,64,64]{2,1,0:T(8,128)(2,1)}, u32[]{:S(2)}) copy-start(bf16[3,64,64]{2,1,0:T(8,128)(2,1)} %param.33) | copy-start | bytes 73732
  76.3 6.2 %collective-permute-start.4 = (bf16[4,1,64,258]{3,2,1,0:T(8,128)(2,1)S(1)}, bf16[4,1,64,258]{3,2,1,0:T(8,128)(2,1)S(1)}, u32[]{:S(2)}, u32[]{:S(2)}) collective-permute-start(bf16[4,1,64,258]{3,2,1,0:T(8,128)(2,1)S(1)} %get-tuple-element.159), channel_id=1, source_target_pairs={{1,0},{2,1},{3,2},{4,3},{5,4},{6,5},{7,6},{9,8},{10,9},{11,10},{12... | collective-permute-start | bytes 396296 | tf_op jit(solution)/shard_map/ppermute | solution.py:23
  77.7 4.8 %collective-permute-start.5 = (bf16[4,1,64,258]{3,2,1,0:T(8,128)(2,1)S(1)}, bf16[4,1,64,258]{3,2,1,0:T(8,128)(2,1)S(1)}, u32[]{:S(2)}, u32[]{:S(2)}) collective-permute-start(bf16[4,1,64,258]{3,2,1,0:T(8,128)(2,1)S(1)} %get-tuple-element.160), channel_id=1, source_target_pairs={{0,1},{1,2},{2,3},{3,4},{4,5},{5,6},{6,7},{8,9},{9,10},{10,11},{11... | collective-permute-start | bytes 396296 | tf_op jit(solution)/shard_map/ppermute | solution.py:22
  131.2 3.0 copy-start.4
  134.2 2.9 copy-start.2
  137.1 10.3 %copy-start.11 = (bf16[4,4,64,256]{3,2,1,0:T(8,128)(2,1)S(1)}, bf16[4,4,64,256]{3,2,1,0:T(8,128)(2,1)}, u32[]{:S(2)}) copy-start(bf16[4,4,64,256]{3,2,1,0:T(8,128)(2,1)} %get-tuple-element.167) | copy-start | bytes 1572868
  140.4 127.0 %collective-permute-start.6 = (bf16[4,64,258]{2,1,0:T(8,128)(2,1)}, bf16[4,64,258]{2,1,0:T(8,128)(2,1)}, u32[]{:S(2)}, u32[]{:S(2)}) collective-permute-start(bf16[4,64,258]{2,1,0:T(8,128)(2,1)} %get-tuple-element.156), channel_id=1, source_target_pairs={{0,1},{1,2},{2,3},{3,4},{4,5},{5,6},{6,7},{8,9},{9,10},{10,11},{11... | collective-permute-start | bytes 396296 | tf_op jit(solution)/shard_map/ppermute | solution.py:31
  144.8 125.8 %collective-permute-start.7 = (bf16[4,64,258]{2,1,0:T(8,128)(2,1)}, bf16[4,64,258]{2,1,0:T(8,128)(2,1)}, u32[]{:S(2)}, u32[]{:S(2)}) collective-permute-start(bf16[4,64,258]{2,1,0:T(8,128)(2,1)} %get-tuple-element.155), channel_id=1, source_target_pairs={{1,0},{2,1},{3,2},{4,3},{5,4},{6,5},{7,6},{9,8},{10,9},{11,10},{12... | collective-permute-start | bytes 396296 | tf_op jit(solution)/shard_map/ppermute | solution.py:31
  273.0 4.3 %collective-permute-start.8 = (bf16[4,32,64]{2,0,1:T(4,128)(2,1)S(1)}, bf16[4,32,64]{2,0,1:T(4,128)(2,1)S(1)}, u32[]{:S(2)}, u32[]{:S(2)}) collective-permute-start(bf16[4,32,64]{2,0,1:T(4,128)(2,1)S(1)} %convert_element_type.38), channel_id=1, source_target_pairs={{8,0},{0,8},{9,1},{1,9},{10,2},{2,10},{11,3},{3,11},{12,4},{4,12},... | collective-permute-start | bytes 49160 | tf_op jit(solution)/shard_map/ppermute | solution.py:12
  275.2 4.0 %collective-permute-start.9 = (bf16[4,32,64]{2,0,1:T(4,128)(2,1)S(1)}, bf16[4,32,64]{2,0,1:T(4,128)(2,1)S(1)}, u32[]{:S(2)}, u32[]{:S(2)}) collective-permute-start(bf16[4,32,64]{2,0,1:T(4,128)(2,1)S(1)} %convert_element_type.39), channel_id=1, source_target_pairs={{8,0},{0,8},{9,1},{1,9},{10,2},{2,10},{11,3},{3,11},{12,4},{4,12},... | collective-permute-start | bytes 49160 | tf_op jit(solution)/shard_map/ppermute | solution.py:12
  (5 other events, 8.1 us)
Sparse Core Ops, SparseCore 0:
  137.3 128.2 all-reduce.5
where the time goes:
time: 318 us; the launch traced here: 317 us
  blocking collectives  120 us (38%)
  waiting for transfers between devices  74.3 us (23%)
  local copies, waits for them, and re-layouts  49.8 us (16%)
  matrix products  27.6 us (9%)
  starting transfers between devices  20.2 us (6%)
  between operations  15.2 us (5%)
  other arithmetic  9.59 us (3%)
    psum x1, waiting for transfers between devices, shards(): lax.psum((hex_local, time_local), ('tm', 'diamond', 'tile'))  71.3 us
    psum x1, blocking collectives, shards(): lax.psum((hex_local, time_local), ('tm', 'diamond', 'tile'))  45.7 us
    scatter-add x5, local copies, waits for them, and re-layouts, shards(): spread = spread.at[:, 1 + step_row:1 + step_row + tile_rows, :, 1 + step_...  30.8 us
    unnamed x1, blocking collectives  26.9 us
    all_gather x1, blocking collectives, shards(): lax.all_gather(field[..., 0], 'tile', axis=1, tiled=True)  25.1 us
    all_gather x1, blocking collectives, shards(): lax.all_gather(field[..., columns - 1], 'tile', axis=1, tiled=True)  22.7 us
    dot_general x7, matrix products, shards(): jnp.einsum('frdx,cd->frcx', grad_wide, hex_weight[number], preferred_elem...  9.43 us
    ppermute x2, starting transfers between devices, with_halo(): before = lax.ppermute(last, axis, up)  7.4 us
  transfers between devices with their start and end apart: 11, of which 3 were waited for; matrix products, arithmetic and copies ran while one was open for 9% of the time, Pallas kernels for 0%

commit v1 on v0

--- a/solution.py
+++ b/solution.py
@@ -4,6 +4,28 @@
 from jax.sharding import PartitionSpec as P
 
 OFFSETS = ((0, 0), (0, 1), (0, -1), (1, 0), (-1, 0), (1, -1), (-1, 1))
+
+
+def in_order(tiles, dim):
+    tiles = jnp.moveaxis(tiles, 0, dim)
+    lengths = tiles.shape
+    return tiles.reshape(*lengths[:dim], lengths[dim] * lengths[dim + 1], *lengths[dim + 2 :])
+
+
+def collected_by_bits(shard, axis):
+    size = lax.axis_size(axis)
+    blocks = shard[None]
+    for level in range(size.bit_length() - 1):
+        bit = 1 << level
+        other = lax.ppermute(blocks, axis, [(i, i ^ bit) for i in range(size)])
+        both = jnp.stack([blocks, other])
+        upper = lax.axis_index(axis) >> level & 1
+        blocks = jnp.where(upper == 0, both, both[::-1]).reshape(-1, *shard.shape)
+    return blocks
+
+
+def gather_by_bits(x, axis, dim):
+    return in_order(collected_by_bits(x, axis), dim)
 
 
 def from_behind(block, axis, distance):
@@ -46,7 +68,7 @@
     own_left = lax.dynamic_slice(left_map, (chart, first_row), (1, tile_rows))[0]
     own_right = lax.dynamic_slice(right_map, (chart, first_row), (1, tile_rows))[0]
     strips = (
-        lax.all_gather(field[..., 0], "tile", axis=1, tiled=True),
+        gather_by_bits(field[..., 0], "tile", 1),
         lax.all_gather(field[..., columns - 1], "tile", axis=1, tiled=True),
     )
     prev_right = from_behind(strips[1], "diamond", 1)

time: 318 us -> 306 us (0.962)
  blocking collectives: 120 us -> 96.8 us
  waiting for transfers between devices: 74.3 us -> 80.8 us
  starting transfers between devices: 20.2 us -> 23.5 us
    all_gather x1 -> x0, blocking collectives: 25.1 us -> none  [shards(): lax.all_gather(field[..., 0], 'tile', axis=1, tiled=True)]
    ppermute x0 -> x3, waiting for transfers between devices: none -> 4 us  [collected_by_bits(): other = lax.ppermute(blocks, axis, [(i, i ^ bit) for i in range(size)])]
    ppermute x0 -> x3, starting transfers between devices: none -> 3.58 us  [collected_by_bits(): other = lax.ppermute(blocks, axis, [(i, i ^ bit) for i in range(size)])]
  transfers between devices with their start and end apart: 11 -> 14, of which waited for: 3 -> 6; matrix products, arithmetic and copies ran while one was open for 9% -> 10% of each run, Pallas kernels for 0% -> 0%
where the time goes in v1:
time: 306 us; the launch traced here: 305 us
  blocking collectives  96.8 us (32%)
  waiting for transfers between devices  80.8 us (26%)
  local copies, waits for them, and re-layouts  49.7 us (16%)
  matrix products  29.6 us (10%)
  starting transfers between devices  23.5 us (8%)
  between operations  15.2 us (5%)
  other arithmetic  9.74 us (3%)
    psum x1, waiting for transfers between devices, shards(): lax.psum((hex_local, time_local), ('tm', 'diamond', 'tile'))  71.6 us
    psum x1, blocking collectives, shards(): lax.psum((hex_local, time_local), ('tm', 'diamond', 'tile'))  45.1 us
    scatter-add x5, local copies, waits for them, and re-layouts, shards(): spread = spread.at[:, 1 + step_row:1 + step_row + tile_rows, :, 1 + step_...  30.9 us
    unnamed x1, blocking collectives  26.9 us
    all_gather x1, blocking collectives, shards(): lax.all_gather(field[..., columns - 1], 'tile', axis=1, tiled=True)  24.8 us
    dot_general x7, matrix products, shards(): jnp.einsum('frdx,cd->frcx', grad_wide, hex_weight[number], preferred_elem...  9.58 us
    ppermute x2, starting transfers between devices, with_halo(): before = lax.ppermute(last, axis, up)  7.42 us
    dot_general x7, matrix products, shards(): jnp.einsum('frcx,frdx->cd', window, grad_wide, preferred_element_type=jnp...  6.82 us
  transfers between devices with their start and end apart: 14, of which 6 were waited for; matrix products, arithmetic and copies ran while one was open for 10% of the time, Pallas kernels for 0%

profile of v1, /device:TPU:0, one launch (start us, length us, event | category | flops | bytes accessed | tf_op | source)
XLA Modules:
  0.0 305.3 jit_solution(10522649605461534815)
XLA Ops:
  9.1 24.8 %all-gather = bf16[4,32,64,1]{3,2,1,0:T(8,128)(2,1)S(1)} all-gather(bf16[4,4,64,1]{3,2,1,0:T(8,128)(2,1)S(1)} %get-tuple-element.163), channel_id=2, replica_groups=mesh['tm'=2,'diamond'=2,'tile'=8] {'tile'}, dimensions={1}, use_global_device_ids=true | all-gather | bytes 18432 | tf_op jit(solution)/shard_map/all_gather | solution.py:72
  34.9 1.6 collective-permute-start.6
  37.2 4.1 %collective-permute-start.1 = (bf16[1,4,64,256]{3,2,1,0:T(8,128)(2,1)}, bf16[1,4,64,256]{3,2,1,0:T(8,128)(2,1)}, u32[]{:S(2)}, u32[]{:S(2)}) collective-permute-start(bf16[1,4,64,256]{3,2,1,0:T(8,128)(2,1)} %get-tuple-element.162), channel_id=1, source_target_pairs={{0,16},{1,17},{2,18},{3,19},{4,20},{5,21},{6,22},{7,23},{8,24},{9,... | collective-permute-start | bytes 393224 | tf_op jit(solution)/shard_map/ppermute | solution.py:44
  42.7 2.0 convolution_bitcast_fusion.16
  45.9 2.7 and_reduce_fusion
  49.9 2.5 collective-permute-done.3
  52.5 1.9 collective-permute-start.4
  59.2 2.1 collective-permute-done.5
  66.0 3.4 %collective-permute-start.8 = (bf16[4,1,64,258]{3,2,1,0:T(8,128)(2,1)S(1)}, bf16[4,1,64,258]{3,2,1,0:T(8,128)(2,1)S(1)}, u32[]{:S(2)}, u32[]{:S(2)}) collective-permute-start(bf16[4,1,64,258]{3,2,1,0:T(8,128)(2,1)S(1)} %get-tuple-element.160), channel_id=1, source_target_pairs={{0,1},{1,2},{2,3},{3,4},{4,5},{5,6},{6,7},{8,9},{9,10},{10,11},{11... | collective-permute-start | bytes 396296 | tf_op jit(solution)/shard_map/ppermute | solution.py:44
  79.0 7.1 %scatter-add.39 = f32[4,6,64,258]{3,2,0,1:T(8,128)S(1)} dynamic-update-slice(f32[4,6,64,258]{3,2,0,1:T(8,128)S(1)} %scatter-add.36, f32[4,4,64,256]{3,2,0,1:T(8,128)} %fusion.9, s32[]{:T(128)} %constant.334.clone.1, s32[]{:T(128)} %constant.333.clone.1, s32[]{:T(128)} %constant.334.clone.1, s32[]{:T(128)} %constant.332.clone.1) | dynamic-update-slice | bytes 2097156 | tf_op jit(solution)/shard_map/scatter-add | solution.py:115
  87.8 7.1 %scatter-add.41 = f32[4,6,64,258]{3,2,0,1:T(8,128)S(1)} dynamic-update-slice(f32[4,6,64,258]{3,2,0,1:T(8,128)S(1)} %fusion.11, f32[4,4,64,256]{3,2,0,1:T(8,128)} %fusion.12, s32[]{:T(128)} %constant.334.clone.1, s32[]{:T(128)} %constant.332.clone.1, s32[]{:T(128)} %constant.334.clone.1, s32[]{:T(128)} %constant.333.clone.1) | dynamic-update-slice | bytes 2097156 | tf_op jit(solution)/shard_map/scatter-add | solution.py:115
  94.8 2.7 add_select_fusion.1
  97.5 7.8 %scatter-add.44 = f32[4,6,64,258]{3,2,0,1:T(8,128)S(1)} dynamic-update-slice(f32[4,6,64,258]{3,2,0,1:T(8,128)S(1)} %scatter-add.41, f32[4,4,64,256]{3,2,0,1:T(8,128)} %add_select_fusion.1, s32[]{:T(128)} %constant.334.clone.1, s32[]{:T(128)S(1)} %bitcast.387, s32[]{:T(128)} %constant.334.clone.1, s32[]{:T(128)} %bitcast.70) | dynamic-update-slice | bytes 2097156 | tf_op jit(solution)/shard_map/scatter-add | solution.py:115
  105.6 3.3 %add_select_fusion = f32[4,4,64,256]{3,2,0,1:T(8,128)} fusion(f32[4,6,64,258]{3,2,0,1:T(8,128)S(1)} %fusion.14, s32[]{:T(128)} %bitcast.75, s32[]{:T(128)} %bitcast.76, pred[]{:T(512)} %get-tuple-element.147, bf16[4,4,64,256]{3,2,1,0:T(8,128)(2,1)S(1)} %fusion.15, bf16[7,64,64]{2,1,0:T(8,128)(2,1)S(1)} %copy-done.14), kind=kOutput, calls=%fused_computation.4 | convolution fusion | flops 34078720 | bytes 2637833 | tf_op jit(solution)/shard_map/frdx,cd->frcx/dot_general | solution.py:116
  108.9 8.4 %scatter-add.46 = f32[4,6,64,258]{3,2,0,1:T(8,128)S(1)} dynamic-update-slice(f32[4,6,64,258]{3,2,0,1:T(8,128)S(1)} %fusion.14, f32[4,4,64,256]{3,2,0,1:T(8,128)} %add_select_fusion, s32[]{:T(128)} %constant.334.clone.1, s32[]{:T(128)} %bitcast.75, s32[]{:T(128)} %constant.334.clone.1, s32[]{:T(128)} %bitcast.76) | dynamic-update-slice | bytes 2097156 | tf_op jit(solution)/shard_map/scatter-add | solution.py:115
  125.8 1.9 slice_bitcast_fusion.1
  127.7 4.1 %collective-permute-start.9 = (bf16[4,64,258]{2,1,0:T(8,128)(2,1)}, bf16[4,64,258]{2,1,0:T(8,128)(2,1)}, u32[]{:S(2)}, u32[]{:S(2)}) collective-permute-start(bf16[4,64,258]{2,1,0:T(8,128)(2,1)} %get-tuple-element.156), channel_id=1, source_target_pairs={{0,1},{1,2},{2,3},{3,4},{4,5},{5,6},{6,7},{8,9},{9,10},{10,11},{11... | collective-permute-start | bytes 396296 | tf_op jit(solution)/shard_map/ppermute | solution.py:53
  137.0 45.1 %psum.15 = f32[3,64,64]{2,1,0:T(8,128)} all-reduce(f32[3,64,64]{2,1,0:T(8,128)S(1)} %pad_maximum_fusion.16), channel_id=1, replica_groups=mesh['tm'=2,'diamond'=2,'tile'=8] {'tm','diamond','tile'}, use_global_device_ids=true, to_apply=%region_7.9 | all-reduce | flops 12288 | bytes 98304 | tf_op jit(solution)/shard_map/psum | solution.py:154
  182.1 71.6 %all-reduce.6.cloned.1.call-done = f32[7,64,64]{1,2,0:T(8,128)} async-done(((f32[7,64,64]{1,2,0:T(8,128)}), f32[7,64,64]{1,2,0:T(8,128)}) %all-reduce.6.cloned.1.call-update) | async-done | bytes 114704 | tf_op jit(solution)/shard_map/psum | solution.py:154
  253.7 1.8 copy.135
  255.5 1.7 fusion.33
  265.3 1.9 collective-permute-done.12
  267.3 26.9 %all-reduce.3 = (bf16[4,32,64]{2,0,1:T(4,128)(2,1)S(1)}, bf16[4,32,64]{2,0,1:T(4,128)(2,1)S(1)}) all-reduce(bf16[4,32,64]{2,0,1:T(4,128)(2,1)S(1)} %collective-permute-done.11, bf16[4,32,64]{2,0,1:T(4,128)(2,1)S(1)} %collective-permute-done.12), channel_id=3, replica_groups=mesh['tm'=2,'diamond'=2,'tile'=8] {'tile'}, use_global_device_ids=true, to_apply=%region_3.5.clone | all-reduce | flops 16384 | bytes 65536
  295.0 1.9 scatter-add.51
  (140 shorter events, 51.8 us)
Async XLA Ops:
  7.2 246.6 %all-reduce.6.cloned.1.call-start = ((), (), s32[]{:S(2)}) async-start(), calls=%async_computation | async-start | bytes 458752 | tf_op jit(solution)/shard_map/psum | solution.py:154
  8.5 40.1 %collective-permute-start.2 = (bf16[1,4,4,64]{3,2,1,0:T(4,128)(2,1)S(1)}, bf16[1,4,4,64]{3,2,1,0:T(4,128)(2,1)S(1)}, u32[]{:S(2)}, u32[]{:S(2)}) collective-permute-start(bf16[1,4,4,64]{3,2,1,0:T(4,128)(2,1)S(1)} %bitcast.381), channel_id=1, source_target_pairs={{0,1},{1,0},{2,3},{3,2},{4,5},{5,4},{6,7},{7,6},{8,9},{9,8},{10,11... | collective-permute-start | bytes 6152 | tf_op jit(solution)/shard_map/ppermute | solution.py:20
  9.1 27.4 %copy-start.1 = (bf16[4,1,4,64,256]{4,3,2,1,0:T(8,128)(2,1)S(1)}, bf16[4,1,4,64,256]{4,3,2,1,0:T(8,128)(2,1)}, u32[]{:S(2)}) copy-start(bf16[4,1,4,64,256]{4,3,2,1,0:T(8,128)(2,1)} %param.31) | copy-start | bytes 1572868
  9.1 33.5 %copy-start.16 = (s32[2,32]{1,0:T(2,128)S(1)}, s32[2,32]{1,0:T(2,128)}, u32[]{:S(2)}) copy-start(s32[2,32]{1,0:T(2,128)} %param.35) | copy-start | bytes 772
  33.8 12.1 %copy-start.18 = (s32[4]{0:T(128)S(1)}, s32[4]{0:T(128)}, u32[]{:S(2)}) copy-start(s32[4]{0:T(128)} %constant.341.clone.1) | copy-start | bytes 52
  33.8 14.8 %copy-start.17 = (s32[2,32]{1,0:T(2,128)S(1)}, s32[2,32]{1,0:T(2,128)}, u32[]{:S(2)}) copy-start(s32[2,32]{1,0:T(2,128)} %param.34) | copy-start | bytes 772
  33.8 20.6 %copy-start.19 = (u32[32]{0:T(128)S(1)}, u32[32]{0:T(128)}, u32[]{:S(2)}) copy-start(u32[32]{0:T(128)} %constant.351) | copy-start | bytes 388
  34.9 23.9 %copy-start = (bf16[4,1,4,64,256]{4,3,2,1,0:T(8,128)(2,1)S(1)}, bf16[4,1,4,64,256]{4,3,2,1,0:T(8,128)(2,1)}, u32[]{:S(2)}) copy-start(bf16[4,1,4,64,256]{4,3,2,1,0:T(8,128)(2,1)} %param.30) | copy-start | bytes 1572868
  34.9 23.9 %copy-start.14 = (bf16[7,64,64]{2,1,0:T(8,128)(2,1)S(1)}, bf16[7,64,64]{2,1,0:T(8,128)(2,1)}, u32[]{:S(2)}) copy-start(bf16[7,64,64]{2,1,0:T(8,128)(2,1)} %param.32) | copy-start | bytes 172036
  34.9 23.0 %collective-permute-start.6 = (bf16[4,32,64]{2,0,1:T(4,128)(2,1)S(1)}, bf16[4,32,64]{2,0,1:T(4,128)(2,1)S(1)}, u32[]{:S(2)}, u32[]{:S(2)}) collective-permute-start(bf16[4,32,64]{2,0,1:T(4,128)(2,1)S(1)} %bitcast.376), channel_id=1, source_target_pairs={{8,0},{0,8},{9,1},{1,9},{10,2},{2,10},{11,3},{3,11},{12,4},{4,12},... | collective-permute-start | bytes 49160 | tf_op jit(solution)/shard_map/ppermute | solution.py:34
  37.2 32.5 %collective-permute-start.1 = (bf16[1,4,64,256]{3,2,1,0:T(8,128)(2,1)}, bf16[1,4,64,256]{3,2,1,0:T(8,128)(2,1)}, u32[]{:S(2)}, u32[]{:S(2)}) collective-permute-start(bf16[1,4,64,256]{3,2,1,0:T(8,128)(2,1)} %get-tuple-element.162), channel_id=1, source_target_pairs={{0,16},{1,17},{2,18},{3,19},{4,20},{5,21},{6,22},{7,23},{8,24},{9,... | collective-permute-start | bytes 393224 | tf_op jit(solution)/shard_map/ppermute | solution.py:44
  41.3 33.2 %collective-permute-start = (bf16[1,4,64,256]{3,2,1,0:T(8,128)(2,1)}, bf16[1,4,64,256]{3,2,1,0:T(8,128)(2,1)}, u32[]{:S(2)}, u32[]{:S(2)}) collective-permute-start(bf16[1,4,64,256]{3,2,1,0:T(8,128)(2,1)} %get-tuple-element.161), channel_id=1, source_target_pairs={{16,0},{17,1},{18,2},{19,3},{20,4},{21,5},{22,6},{23,7},{24,8},{25... | collective-permute-start | bytes 393224 | tf_op jit(solution)/shard_map/ppermute | solution.py:45
  48.7 3.7 %collective-permute-start.3 = (bf16[2,4,4,64]{3,2,1,0:T(4,128)(2,1)S(1)}, bf16[2,4,4,64]{3,2,1,0:T(4,128)(2,1)S(1)}, u32[]{:S(2)}, u32[]{:S(2)}) collective-permute-start(bf16[2,4,4,64]{3,2,1,0:T(4,128)(2,1)S(1)} %get-tuple-element.166), channel_id=1, source_target_pairs={{0,2},{1,3},{2,0},{3,1},{4,6},{5,7},{6,4},{7,5},{8,10},{9,11},{10,... | collective-permute-start | bytes 12296 | tf_op jit(solution)/shard_map/ppermute | solution.py:20
  52.5 4.7 %collective-permute-start.4 = (bf16[4,4,4,64]{3,2,1,0:T(4,128)(2,1)S(1)}, bf16[4,4,4,64]{3,2,1,0:T(4,128)(2,1)S(1)}, u32[]{:S(2)}, u32[]{:S(2)}) collective-permute-start(bf16[4,4,4,64]{3,2,1,0:T(4,128)(2,1)S(1)} %bitcast.374), channel_id=1, source_target_pairs={{0,4},{1,5},{2,6},{3,7},{4,0},{5,1},{6,2},{7,3},{8,12},{9,13},{10,... | collective-permute-start | bytes 24584 | tf_op jit(solution)/shard_map/ppermute | solution.py:20
  57.3 4.0 %collective-permute-start.5 = (bf16[4,32,64]{2,0,1:T(4,128)(2,1)S(1)}, bf16[4,32,64]{2,0,1:T(4,128)(2,1)S(1)}, u32[]{:S(2)}, u32[]{:S(2)}) collective-permute-start(bf16[4,32,64]{2,0,1:T(4,128)(2,1)S(1)} %copy.92), channel_id=1, source_target_pairs={{8,0},{0,8},{9,1},{1,9},{10,2},{2,10},{11,3},{3,11},{12,4},{4,12},... | collective-permute-start | bytes 49160 | tf_op jit(solution)/shard_map/ppermute | solution.py:34
  58.8 12.2 %copy-start.7 = (bf16[4,4,64,1]{3,2,1,0:T(8,128)(2,1)}, bf16[4,4,64,1]{3,2,1,0:T(8,128)(2,1)S(1)}, u32[]{:S(2)}) copy-start(bf16[4,4,64,1]{3,2,1,0:T(8,128)(2,1)S(1)} %copy.98) | copy-start | bytes 6148
  64.6 6.3 %collective-permute-start.7 = (bf16[4,1,64,258]{3,2,1,0:T(8,128)(2,1)S(1)}, bf16[4,1,64,258]{3,2,1,0:T(8,128)(2,1)S(1)}, u32[]{:S(2)}, u32[]{:S(2)}) collective-permute-start(bf16[4,1,64,258]{3,2,1,0:T(8,128)(2,1)S(1)} %get-tuple-element.159), channel_id=1, source_target_pairs={{1,0},{2,1},{3,2},{4,3},{5,4},{6,5},{7,6},{9,8},{10,9},{11,10},{12... | collective-permute-start | bytes 396296 | tf_op jit(solution)/shard_map/ppermute | solution.py:45
  66.0 4.9 %collective-permute-start.8 = (bf16[4,1,64,258]{3,2,1,0:T(8,128)(2,1)S(1)}, bf16[4,1,64,258]{3,2,1,0:T(8,128)(2,1)S(1)}, u32[]{:S(2)}, u32[]{:S(2)}) collective-permute-start(bf16[4,1,64,258]{3,2,1,0:T(8,128)(2,1)S(1)} %get-tuple-element.160), channel_id=1, source_target_pairs={{0,1},{1,2},{2,3},{3,4},{4,5},{5,6},{6,7},{8,9},{9,10},{10,11},{11... | collective-permute-start | bytes 396296 | tf_op jit(solution)/shard_map/ppermute | solution.py:44
  122.9 10.2 %copy-start.2 = (bf16[4,1,4,64,256]{4,3,2,1,0:T(8,128)(2,1)S(1)}, bf16[4,1,4,64,256]{4,3,2,1,0:T(8,128)(2,1)}, u32[]{:S(2)}) copy-start(bf16[4,1,4,64,256]{4,3,2,1,0:T(8,128)(2,1)} %param.31) | copy-start | bytes 1572868
  125.8 10.0 %copy-start.12 = (bf16[4,4,64,256]{3,2,1,0:T(8,128)(2,1)S(1)}, bf16[4,4,64,256]{3,2,1,0:T(8,128)(2,1)}, u32[]{:S(2)}) copy-start(bf16[4,4,64,256]{3,2,1,0:T(8,128)(2,1)} %get-tuple-element.169) | copy-start | bytes 1572868
  127.7 127.8 %collective-permute-start.9 = (bf16[4,64,258]{2,1,0:T(8,128)(2,1)}, bf16[4,64,258]{2,1,0:T(8,128)(2,1)}, u32[]{:S(2)}, u32[]{:S(2)}) collective-permute-start(bf16[4,64,258]{2,1,0:T(8,128)(2,1)} %get-tuple-element.156), channel_id=1, source_target_pairs={{0,1},{1,2},{2,3},{3,4},{4,5},{5,6},{6,7},{8,9},{9,10},{10,11},{11... | collective-permute-start | bytes 396296 | tf_op jit(solution)/shard_map/ppermute | solution.py:53
  131.8 126.9 %collective-permute-start.10 = (bf16[4,64,258]{2,1,0:T(8,128)(2,1)}, bf16[4,64,258]{2,1,0:T(8,128)(2,1)}, u32[]{:S(2)}, u32[]{:S(2)}) collective-permute-start(bf16[4,64,258]{2,1,0:T(8,128)(2,1)} %get-tuple-element.155), channel_id=1, source_target_pairs={{1,0},{2,1},{3,2},{4,3},{5,4},{6,5},{7,6},{9,8},{10,9},{11,10},{12... | collective-permute-start | bytes 396296 | tf_op jit(solution)/shard_map/ppermute | solution.py:53
  261.1 4.3 %collective-permute-start.11 = (bf16[4,32,64]{2,0,1:T(4,128)(2,1)S(1)}, bf16[4,32,64]{2,0,1:T(4,128)(2,1)S(1)}, u32[]{:S(2)}, u32[]{:S(2)}) collective-permute-start(bf16[4,32,64]{2,0,1:T(4,128)(2,1)S(1)} %convert_element_type.38), channel_id=1, source_target_pairs={{8,0},{0,8},{9,1},{1,9},{10,2},{2,10},{11,3},{3,11},{12,4},{4,12},... | collective-permute-start | bytes 49160 | tf_op jit(solution)/shard_map/ppermute | solution.py:34
  263.3 4.0 %collective-permute-start.12 = (bf16[4,32,64]{2,0,1:T(4,128)(2,1)S(1)}, bf16[4,32,64]{2,0,1:T(4,128)(2,1)S(1)}, u32[]{:S(2)}, u32[]{:S(2)}) collective-permute-start(bf16[4,32,64]{2,0,1:T(4,128)(2,1)S(1)} %convert_element_type.39), channel_id=1, source_target_pairs={{8,0},{0,8},{9,1},{1,9},{10,2},{2,10},{11,3},{3,11},{12,4},{4,12},... | collective-permute-start | bytes 49160 | tf_op jit(solution)/shard_map/ppermute | solution.py:34
  (10 other events, 23.4 us)
Sparse Core Ops, SparseCore 0:
  125.9 127.7 all-reduce.5
